TPU v7x, 256 devices: a whole 4x4x8 slice. The times are simulated.
256 devices in a mesh: dp: 32 (over x, z), mp: 8 (over y, core).
Axes of the slice: x: 4, y: 4, z: 8, core: 2. Of those that a mesh axis runs over, the one named last changes fastest.
Arguments:
- grads: bfloat16 [32768, 16384], P('dp', 'mp'), may hold values from -6 to 6
- scales: float32 [128, 32768], P('mp', 'dp'), may hold values from 0.25 to 4
- example_group: int32 [32, 1024], P('dp'), may hold values from 0 to 127, never falling along the last dimension, each value on 1 to 32 neighbouring positions
- group_slot: int32 [4096], P('dp'), may hold values from 0 to 4095, as said below
- inv_hess: bfloat16 [16384, 16384], P('mp', 'dp'), may hold values from -0.046875 to 0.046875
- queries: bfloat16 [1024, 16384], P(None, 'mp'), may hold values from -0.029907227 to 0.029907227
Outputs:
- scores: float32 [4096, 1024], P('dp', 'mp')
Inputs may be any that keep to these rules, and one draw needn't show every extreme that they name: `group_slot`: A permutation of the 4096 rows. The groups of one block of 128 (one index of dp) put at most 8 groups into the rows of any one owner block of 128 output rows, and exactly 8 into some owner block.
All inputs are finite; a program needn't handle non-finite values.
Results may differ from a plain program's by a relative error of at most 0.0049.
Values may be sent and summed in bfloat16 or wider, within the bound.
A program may use at most 64 MiB of HBM per device.

v0:
```python
import jax
import jax.numpy as jnp
from jax import lax
from jax.sharding import PartitionSpec as P

QBLOCK = 128
GRP_DEV = 128


def split_up(value, dim, peers):
    before, after = (value.shape[:dim], value.shape[dim + 1 :])
    return jnp.moveaxis(value.reshape(*before, peers, -1, *after), dim, 0)


def sum_at_owner(value, axis, dim):
    peers = lax.axis_size(axis)
    parts = lax.all_to_all(split_up(value, dim, peers), axis, 0, 0, tiled=True)
    return jnp.sum(parts, axis=0)


def joined_along(parts, dim):
    parts = jnp.moveaxis(parts, 0, dim)
    dims = parts.shape
    return parts.reshape(*dims[:dim], dims[dim] * dims[dim + 1], *dims[dim + 2 :])


def copy_for_each(value, axis):
    copies = jnp.broadcast_to(value, (lax.axis_size(axis), *value.shape))
    return lax.all_to_all(copies, axis, split_axis=0, concat_axis=0, tiled=True)


def gather_directly(value, axis, dim):
    return joined_along(copy_for_each(value, axis), dim)


def spread_2(value, axis, source):
    kept = jnp.where(lax.axis_index(axis) == source, value, 0).astype(value.dtype)
    return lax.psum(kept, axis)


def in_one_piece(arrays, axis, split_dim, concat_dim, along):
    columns = [a.reshape(*a.shape[:along], -1) for a in arrays]
    both = jnp.concatenate(columns, axis=along)
    whole, at, finished = (
        lax.all_to_all(both, axis, split_axis=split_dim, concat_axis=concat_dim, tiled=True),
        0,
        [],
    )
    for a, column in zip(arrays, columns):
        slab = whole[..., at : at + column.shape[along]]
        finished.append(slab.reshape(*slab.shape[:along], *a.shape[along:]))
        at += column.shape[along]
    return tuple(finished)


def contract(left, right):
    return lax.dot_general(
        left, right, (((1,), (1,)), ((), ())), preferred_element_type=jnp.float32
    )


def local(grads, scales, example_group, group_slot, inv_hess, queries):
    devices = lax.axis_size("dp")
    lanes = lax.axis_size("mp")
    spread = devices // lanes
    ex_rows, width = grads.shape
    query_count = queries.shape[0]
    share = query_count // lanes
    dequant = (
        (grads.reshape(ex_rows, width // QBLOCK, QBLOCK) * jnp.transpose(scales)[:, :, None])
        .astype(jnp.bfloat16)
        .reshape(ex_rows, width)
    )
    onehot = (jnp.arange(GRP_DEV, dtype=jnp.int32)[:, None] == example_group[0][None, :]).astype(
        jnp.bfloat16
    )
    group_grad = jnp.dot(onehot, dequant, preferred_element_type=jnp.float32).astype(jnp.bfloat16)
    query_block = sum_at_owner(
        jnp.dot(queries, inv_hess, preferred_element_type=jnp.float32), "mp", 0
    ).astype(jnp.bfloat16)
    column_block = gather_directly(query_block, "mp", 0)
    first_root = spread * lax.axis_index("mp")
    received = [spread_2(column_block, "dp", first_root + offset) for offset in range(spread)]
    precond = jnp.concatenate(received, axis=1)
    partial_value = contract(group_grad, precond)
    mine = sum_at_owner(partial_value, "mp", 1)
    owner = group_slot // GRP_DEV
    inside = group_slot % GRP_DEV
    local_index = jnp.arange(GRP_DEV, dtype=jnp.int32)
    earlier = (owner[:, None] == owner[None, :]) & (local_index[None, :] < local_index[:, None])
    order_rank = jnp.sum(earlier.astype(jnp.int32), axis=1)
    capacity = 2 * GRP_DEV // devices
    buffer_row = owner * capacity + order_rank
    outgoing = jnp.zeros((devices * capacity, share), jnp.float32).at[buffer_row].set(mine)
    targets = (
        jnp.full((devices * capacity,), float(GRP_DEV), jnp.float32)
        .at[buffer_row]
        .set(inside.astype(jnp.float32))
    )
    arrived, arrived_rows = in_one_piece(
        (outgoing.reshape(devices, capacity, share), targets.reshape(devices, capacity)),
        "dp",
        0,
        0,
        2,
    )
    place_rows = arrived_rows.reshape(-1).astype(jnp.int32)
    filled = (
        jnp.zeros((GRP_DEV + 1, share), jnp.float32).at[place_rows].add(arrived.reshape(-1, share))
    )
    return filled[:GRP_DEV]


def solution(mesh):
    in_specs = (P("dp", "mp"), P("mp", "dp"), P("dp", None), P("dp"), P("mp", "dp"), P(None, "mp"))
    out_specs = P("dp", "mp")
    return jax.shard_map(local, mesh=mesh, in_specs=in_specs, out_specs=out_specs, check_vma=False)
```

profile of v0, /device:TPU:1, one launch (start us, length us, event | category | flops | bytes accessed | tf_op | source)
XLA Modules:
  0.0 291.3 jit_solution(12097009957942378404)
XLA Ops:
  6.5 1.6 copy-done
  8.1 4.5 %fusion.31 = f32[1024,512]{1,0:T(8,128)S(1)} fusion(bf16[1024,2048]{1,0:T(8,128)(2,1)} %param.11, bf16[2048,512]{1,0:T(8,128)(2,1)S(1)} %copy-done), kind=kOutput, calls=%fused_computation.45 | convolution fusion | flops 2147483648 | bytes 8388608 | tf_op jit(solution)/shard_map/dot_general | solution.py:79
  12.6 32.5 %all_to_all.20 = f32[8,128,512]{2,1,0:T(8,128)} all-to-all(f32[8,128,512]{2,1,0:T(8,128)S(1)} %bitcast.37), channel_id=1, replica_groups=mesh['dp'=32,'mp'=8] {'mp'}, dimensions={0} | all-to-all | bytes 4194304 | tf_op jit(solution)/shard_map/all_to_all | solution.py:17
  45.2 1.8 reduce_sum.28
  47.0 1.1 broadcast_in_dim.33
  48.1 4.5 %all-to-all-start.1 = ((bf16[8,128,512]{2,1,0:T(8,128)(2,1)}), bf16[8,128,512]{2,1,0:T(8,128)(2,1)S(1)}, u32[]{:S(2)}, u32[]{:S(2)}) async-start(bf16[8,128,512]{2,1,0:T(8,128)(2,1)} %broadcast_in_dim.33), calls=%async_computation.1 | async-start | bytes 2097152 | tf_op jit(solution)/shard_map/all_to_all | solution.py:29
  52.6 15.0 %all-to-all-done.1 = bf16[8,128,512]{2,1,0:T(8,128)(2,1)S(1)} async-done(((bf16[8,128,512]{2,1,0:T(8,128)(2,1)}), bf16[8,128,512]{2,1,0:T(8,128)(2,1)S(1)}, u32[]{:S(2)}, u32[]{:S(2)}) %all-to-all-start.1) | async-done | bytes 1048608 | tf_op jit(solution)/shard_map/all_to_all | solution.py:29
  67.6 2.1 broadcast_select_fusion.3
  69.7 0.2 copy.15
  69.9 162.0 %all-reduce.3.cloned.1.call-done = (bf16[1024,512]{1,0:T(8,128)(2,1)}, bf16[1024,512]{1,0:T(8,128)(2,1)}, bf16[1024,512]{1,0:T(8,128)(2,1)}, bf16[1024,512]{1,0:T(8,128)(2,1)}) async-done(((bf16[1024,512]{1,0:T(8,128)(2,1)}, bf16[1024,512]{1,0:T(8,128)(2,1)}, bf16[1024,512]{1,0:T(8,128)(2,1)}, bf16[1024,512]{1,0:T(8,128)(2,1)}), (bf16[1024,512]{1,0:T(8,128)(2,1)}, bf16[1024,512]{1,0:T(8,128)(2,1)}, ...) | async-done | bytes 4194320 | tf_op jit(solution)/shard_map/psum | solution.py:38
  231.8 5.9 %mul.19 = f32[1024,16,128]{2,1,0:T(8,128)} broadcast(f32[1024,16]{1,0:T(8,128)S(1)} %copy.15), dimensions={0,1} | broadcast | bytes 8454144 | tf_op jit(solution)/shard_map/mul | solution.py:70
  237.7 10.0 %fusion.14 = f32[16,8,8,128]{3,2,1,0:T(8,128)S(1)} fusion(bf16[1024,512]{1,0:T(8,128)(2,1)} %get-tuple-element.5, bf16[1024,512]{1,0:T(8,128)(2,1)} %get-tuple-element.6, bf16[1024,512]{1,0:T(8,128)(2,1)} %get-tuple-element.7, bf16[1024,512]{1,0:T(8,128)(2,1)} %get-tuple-element.8, f32[128,8,16,128]{3,2,1,0:T(8,128)} %bitcast.32, ...), kind=kOutput, calls=%fused_computation.15 | convolution fusion | flops 1097203712 | bytes 17305600 | tf_op jit(solution)/shard_map/dot_general | solution.py:57
  247.7 0.8 copy.27
  248.5 7.8 %all-to-all-start.2 = ((f32[8,128,128]{2,1,0:T(8,128)}), f32[8,128,128]{2,1,0:T(8,128)S(1)}, u32[]{:S(2)}, u32[]{:S(2)}) async-start(f32[8,128,128]{2,1,0:T(8,128)} %bitcast.31), calls=%async_computation.2 | async-start | bytes 1048576 | tf_op jit(solution)/shard_map/all_to_all | solution.py:17
  256.4 0.2 convert_reduce_fusion
  256.5 1.0 scatter_custom_fusion.1
  257.5 0.2 reshape_reshape.5
  257.7 7.9 %all-to-all-done.2 = f32[8,128,128]{2,1,0:T(8,128)S(1)} async-done(((f32[8,128,128]{2,1,0:T(8,128)}), f32[8,128,128]{2,1,0:T(8,128)S(1)}, u32[]{:S(2)}, u32[]{:S(2)}) %all-to-all-start.2) | async-done | bytes 524320 | tf_op jit(solution)/shard_map/all_to_all | solution.py:17
  265.7 0.9 scatter_custom_fusion
  266.7 14.8 %all_to_all.21 = f32[32,8,129]{2,1,0:T(8,128)S(1)} all-to-all(f32[32,8,129]{2,1,0:T(8,128)S(1)} %pad_maximum_fusion), channel_id=1, replica_groups=mesh['dp'=32,'mp'=8] {'dp'}, dimensions={0} | all-to-all | bytes 264192 | tf_op jit(solution)/shard_map/all_to_all | solution.py:45
  281.5 0.6 fusion.22
  282.1 0.1 convert_element_type.46
  282.2 1.6 scatter_custom_fusion.2
  283.8 0.6 slice.14
  (14 shorter events, 0.1 us)
Async XLA Ops:
  6.5 1.6 copy-start
  48.1 19.5 %all-to-all-start.1 = ((bf16[8,128,512]{2,1,0:T(8,128)(2,1)}), bf16[8,128,512]{2,1,0:T(8,128)(2,1)S(1)}, u32[]{:S(2)}, u32[]{:S(2)}) async-start(bf16[8,128,512]{2,1,0:T(8,128)(2,1)} %broadcast_in_dim.33), calls=%async_computation.1 | async-start | bytes 2097152 | tf_op jit(solution)/shard_map/all_to_all | solution.py:29
  52.6 179.3 %all-reduce.3.cloned.1.call-start = ((), (), s32[]{:S(2)}) async-start(), calls=%async_computation.4 | async-start | bytes 8388608 | tf_op jit(solution)/shard_map/psum | solution.py:38
  52.6 17.1 %copy-start.1 = (f32[16,1024]{1,0:T(8,128)S(1)}, f32[16,1024]{1,0:T(8,128)}, u32[]{:S(2)}) copy-start(f32[16,1024]{1,0:T(8,128)} %param.7) | copy-start | bytes 196612
  231.8 5.9 %copy-start.2 = (s32[1,1024]{1,0:T(1,128)S(1)}, s32[1,1024]{1,0:T(1,128)}, u32[]{:S(2)}) copy-start(s32[1,1024]{1,0:T(1,128)} %param.8) | copy-start | bytes 12292
  237.7 18.7 %copy-start.3 = (s32[128]{0:T(128)S(1)}, s32[128]{0:T(128)}, u32[]{:S(2)}) copy-start(s32[128]{0:T(128)} %param.9) | copy-start | bytes 1540
  248.5 17.2 %all-to-all-start.2 = ((f32[8,128,128]{2,1,0:T(8,128)}), f32[8,128,128]{2,1,0:T(8,128)S(1)}, u32[]{:S(2)}, u32[]{:S(2)}) async-start(f32[8,128,128]{2,1,0:T(8,128)} %bitcast.31), calls=%async_computation.2 | async-start | bytes 1048576 | tf_op jit(solution)/shard_map/all_to_all | solution.py:17
Sparse Core Ops, SparseCore 0:
  69.8 161.9 all-reduce.2
where the time goes:
time: 294 us; the launch traced here: 291 us
  waiting for transfers between devices  185 us (63%)
  blocking collectives  47.3 us (16%)
  matrix products  14.5 us (5%)
  between operations  13.5 us (5%)
  local copies, waits for them, and re-layouts  12.4 us (4%)
  starting transfers between devices  12.3 us (4%)
  other arithmetic  6.37 us (2%)
    psum x1, waiting for transfers between devices, spread_2(): return lax.psum(kept, axis)  162 us
    all_to_all x1, blocking collectives, sum_at_owner(): parts = lax.all_to_all(split_up(value, dim, peers), axis, 0, 0, tiled=True)  32.5 us
    all_to_all x1, waiting for transfers between devices, copy_for_each(): return lax.all_to_all(copies, axis, split_axis=0, concat_axis=0, tiled=True)  15 us
    all_to_all x1, blocking collectives, in_one_piece(): lax.all_to_all(both, axis, split_axis=split_dim, concat_axis=concat_dim,...  14.8 us
    dot_general x1, matrix products, contract(): lax.dot_general(left, right, (((1,), (1,)), ((), ())), preferred_element_...  9.98 us
    all_to_all x1, waiting for transfers between devices, sum_at_owner(): parts = lax.all_to_all(split_up(value, dim, peers), axis, 0, 0, tiled=True)  7.95 us
    all_to_all x1, starting transfers between devices, sum_at_owner(): parts = lax.all_to_all(split_up(value, dim, peers), axis, 0, 0, tiled=True)  7.84 us
  transfers between devices with their start and end apart: 3, of which 3 were waited for; matrix products, arithmetic and copies ran while one was open for 1% of the time, Pallas kernels for 0%

commit v1 on v0

v1 whole, which is shorter than its diff:
```python
import functools

import jax
import jax.numpy as jnp
from jax import lax
from jax.experimental import pallas as pl
from jax.experimental.pallas import tpu as pltpu
from jax.sharding import PartitionSpec as P

MESH = pl.DeviceIdType.MESH
BF16, F32, I32 = jnp.bfloat16, jnp.float32, jnp.int32
NX, NY, NZ = 4, 4, 8
KCH = 2
CW = 256


def dev(x, y, z, c):
    return (lax.rem(x, NX) * NZ + lax.rem(z, NZ), lax.rem(y, NY) * 2 + c)


def kernel(
    grads_ref, sct_ref, member_ref, slot_ref, hess_ref, query_ref, out_ref,
    q_v, h_v, g_v, ex_s, ex_r, own, rs_s, rs_r, tr_s, pre, gall, acc, slots, slot_rep, pack, place, a2a_s, a2a_r,
    in_sem, ex_sem, rs_sem, rr_sem, tr_sem, agr_sem, agl_sem, gr_sem, gl_sem, gf_sem, gp_sem, sl_sem, slr_sem, as_sem, ar_sem,
):
    d = lax.axis_index("dp")
    m = lax.axis_index("mp")
    x, z = lax.div(d, NZ), lax.rem(d, NZ)
    y, c = lax.div(m, 2), lax.rem(m, 2)
    oc = 1 - c
    beta = lax.rem(2 * y - x + NX, NX)
    stays = (x == y).astype(I32)

    def q_copy(i, b):
        h = oc if i == 0 else c
        rows = pl.ds(pl.multiple_of(b * 256 + h * 128, 128), 128)
        return pltpu.make_async_copy(query_ref.at[rows], q_v.at[i, b], in_sem.at[i * 4 + b])

    def h_copy(k):
        return pltpu.make_async_copy(hess_ref.at[:, pl.ds(k * CW, CW)], h_v.at[k], in_sem.at[8 + k])

    def g_copy(i):
        return pltpu.make_async_copy(grads_ref.at[:, pl.ds(i * 1024, 1024)], g_v.at[i], in_sem.at[10 + i])

    h_copy(0).start()
    for b in range(4):
        q_copy(0, b).start()
    for b in range(4):
        q_copy(1, b).start()
    h_copy(1).start()
    g_copy(0).start()
    g_copy(1).start()

    barrier = pltpu.get_barrier_semaphore()

    def greet(target):
        pl.semaphore_signal(barrier, inc=1, device_id=target, device_id_type=MESH)

    greet(dev(x, y, z, oc))
    for o in (1, 2, 3):
        greet(dev(x, y + o, z, c))
    greet(dev(x + 1, y, z, c))
    greet(dev(x + 3, y, z, c))
    greet(dev(x, y, z + 1, c))
    greet(dev(x, y, z + 7, c))

    def owner_of(o):
        return dev(lax.div(o, NZ), beta, lax.rem(o, NZ), c)

    def source_of(s):
        ys, zs = lax.div(s, NZ), lax.rem(s, NZ)
        return dev(2 * ys - y + NX, ys, zs, c)

    own_src = y * NZ + z
    me_owner = jnp.where(stays == 1, d, -1)
    me_source = jnp.where(stays == 1, own_src, -1)

    def greet_32(i, carry):
        @pl.when(i != me_owner)
        def _():
            greet(owner_of(i))

        @pl.when(i != me_source)
        def _():
            greet(source_of(i))

        return carry

    lax.fori_loop(0, 32, greet_32, 0)

    def partial(i, k):
        return jnp.dot(q_v[i].reshape(512, 2048), h_v[k], preferred_element_type=F32)

    def ex_copy(k):
        return pltpu.make_async_remote_copy(
            src_ref=ex_s.at[k], dst_ref=ex_r.at[k], send_sem=ex_sem.at[0, k], recv_sem=ex_sem.at[1, k],
            device_id=dev(x, y, z, oc), device_id_type=MESH)

    h_copy(0).wait()
    for b in range(4):
        q_copy(0, b).wait()
    ex_s[0] = partial(0, 0).astype(BF16).reshape(4, 128, CW)
    pl.semaphore_wait(barrier, 72 - 2 * stays)
    ex_copy(0).start()
    for b in range(4):
        q_copy(1, b).wait()
    own[0] = partial(1, 0).reshape(4, 128, CW)
    h_copy(1).wait()
    ex_s[1] = partial(0, 1).astype(BF16).reshape(4, 128, CW)
    ex_copy(1).start()

    def rs_copy(k, o):
        b = lax.rem(y + o, NY)
        return pltpu.make_async_remote_copy(
            src_ref=rs_s.at[k, b], dst_ref=rs_r.at[k, y], send_sem=rs_sem.at[k, o], recv_sem=rr_sem.at[k, y],
            device_id=dev(x, y + o, z, c), device_id_type=MESH)

    def rs_wait_recv(k, o):
        s = lax.rem(y + o, NY)
        pltpu.make_async_remote_copy(
            src_ref=rs_s.at[k, s], dst_ref=rs_r.at[k, s], send_sem=rs_sem.at[k, o], recv_sem=rr_sem.at[k, s],
            device_id=dev(x, y + o, z, c), device_id_type=MESH).wait_recv()

    def rs_send(k):
        ex_copy(k).wait_recv()
        for o in (2, 1, 3):
            b = lax.rem(y + o, NY)
            rs_s[k, b] = (own[k, b] + ex_r[k, b].astype(F32)).astype(BF16)
            rs_copy(k, o).start()

    rs_send(0)
    own[1] = partial(1, 1).reshape(4, 128, CW)
    rs_send(1)

    def slot_copy(s):
        return pltpu.make_async_remote_copy(
            src_ref=slot_ref, dst_ref=slots.at[d], send_sem=sl_sem.at[s], recv_sem=slr_sem.at[d],
            device_id=source_of(s), device_id_type=MESH)

    def slot_send(s, carry):
        @pl.when(s != me_source)
        def _():
            slot_copy(s).start()

        return carry

    lax.fori_loop(0, 32, slot_send, 0)

    @pl.when(stays == 1)
    def _():
        slots[d] = slot_ref[...]

    onehot = (lax.broadcasted_iota(I32, (128, 1024), 0) == member_ref[...]).astype(F32).astype(BF16)

    def group_half(h):
        g_copy(h).wait()
        for i in range(2):
            for k in range(KCH):
                col = (i * KCH + k) * CW
                parts = []
                for j in range(2):
                    at = col + j * 128
                    blk = (h * 1024 + at) // 128
                    parts.append((g_v[h, :, at : at + 128].astype(F32) * sct_ref[:, blk : blk + 1]).astype(BF16))
                deq = jnp.concatenate(parts, axis=1)
                gall[x, 4 * c + 2 * h + i, k] = jnp.dot(onehot, deq, preferred_element_type=F32).astype(BF16)

    def piece(xx, cc, h):
        return gall.at[lax.rem(xx, NX), pl.ds(4 * cc + 2 * h, 2)]

    def g_right(h):
        return pltpu.make_async_remote_copy(
            src_ref=piece(x, c, h), dst_ref=piece(x, c, h), send_sem=gr_sem.at[0, h], recv_sem=gr_sem.at[1, h],
            device_id=dev(x + 1, y, z, c), device_id_type=MESH)

    def g_left(h):
        return pltpu.make_async_remote_copy(
            src_ref=piece(x, c, h), dst_ref=piece(x, c, h), send_sem=gl_sem.at[0, h], recv_sem=gl_sem.at[1, h],
            device_id=dev(x + 3, y, z, c), device_id_type=MESH)

    def g_forward(h):
        src = piece(x + 3, c, 0) if h == 0 else piece(x + 1, c, 1)
        to = dev(x + 1, y, z, c) if h == 0 else dev(x + 3, y, z, c)
        return pltpu.make_async_remote_copy(
            src_ref=src, dst_ref=src, send_sem=gf_sem.at[0, h], recv_sem=gf_sem.at[1, h], device_id=to, device_id_type=MESH)

    def g_partner(o, h):
        return pltpu.make_async_remote_copy(
            src_ref=piece(x + o, c, h), dst_ref=piece(x + o, c, h), send_sem=gp_sem.at[0, o, h], recv_sem=gp_sem.at[1, o, h],
            device_id=dev(x, y, z, oc), device_id_type=MESH)

    def g_send(h):
        g_right(h).start()
        g_left(h).start()
        g_partner(0, h).start()

    group_half(0)
    g_send(0)

    def tr_copy(k):
        return pltpu.make_async_remote_copy(
            src_ref=tr_s.at[k], dst_ref=pre.at[k, z], send_sem=tr_sem.at[0, k], recv_sem=tr_sem.at[1, k],
            device_id=dev(2 * x - y + NX, x, z, c), device_id_type=MESH)

    def tr_send(k):
        total = own[k, y] + ex_r[k, y].astype(F32)
        for o in (1, 3, 2):
            rs_wait_recv(k, o)
            total += rs_r[k, lax.rem(y + o, NY)].astype(F32)
        tr_s[k] = total.astype(BF16)

        @pl.when(stays == 0)
        def _():
            tr_copy(k).start()

        @pl.when(stays == 1)
        def _():
            pre[k, z] = total.astype(BF16)

    tr_send(0)
    group_half(1)
    tr_send(1)
    g_send(1)

    def ag_copy(k, s, right):
        sems = agr_sem if right else agl_sem
        blk = lax.rem(z - s + NZ, NZ) if right else lax.rem(z + s, NZ)
        return pltpu.make_async_remote_copy(
            src_ref=pre.at[k, blk], dst_ref=pre.at[k, blk], send_sem=sems.at[0, k, s], recv_sem=sems.at[1, k, s],
            device_id=dev(x, y, z + (1 if right else NZ - 1), c), device_id_type=MESH)

    def ag_wait_recv(k, s, right):
        sems = agr_sem if right else agl_sem
        blk = lax.rem(z - s - 1 + NZ, NZ) if right else lax.rem(z + s + 1, NZ)
        pltpu.make_async_remote_copy(
            src_ref=pre.at[k, blk], dst_ref=pre.at[k, blk], send_sem=sems.at[0, k, s], recv_sem=sems.at[1, k, s],
            device_id=dev(x, y, z + (1 if right else NZ - 1), c), device_id_type=MESH).wait_recv()

    def steps(k, right):
        return 4 if (k == 0) == right else 3

    for k in range(KCH):
        @pl.when(stays == 0)
        def _():
            tr_copy(k).wait_recv()

        ag_copy(k, 0, True).start()
        ag_copy(k, 0, False).start()

    upper = (lax.broadcasted_iota(I32, (128, 128), 0) < lax.broadcasted_iota(I32, (128, 128), 1)).astype(F32).astype(BF16)

    def slot_wait(o, carry):
        @pl.when(o != me_owner)
        def _():
            pltpu.make_async_remote_copy(
                src_ref=slot_ref, dst_ref=slots.at[o], send_sem=sl_sem.at[o], recv_sem=slr_sem.at[o],
                device_id=source_of(o), device_id_type=MESH).wait_recv()

        return carry

    lax.fori_loop(0, 32, slot_wait, 0)
    row = lax.broadcasted_iota(I32, (1024, 128), 0)
    for xx in range(NX):
        hit = lax.shift_right_logical(slots[xx * NZ + z], 7) == lax.shift_right_logical(row, 5)
        mine = hit & ((lax.shift_right_logical(row, 3) & 3) == xx)
        rank = jnp.dot(hit.astype(F32).astype(BF16), upper, preferred_element_type=F32)
        pack[:, xx * 128 : (xx + 1) * 128] = jnp.where(
            mine & (rank == (row & 7).astype(F32)), 1.0, 0.0).astype(BF16)
    for j in range(32):
        slot_rep[j * 8 : (j + 1) * 8, :] = jnp.broadcast_to(slots[(j % 4) * NZ + j // 4], (8, 128))
    rep = slot_rep[...]
    row = lax.broadcasted_iota(I32, (256, 128), 0)
    hit = lax.shift_right_logical(rep, 7) == d
    rank = jnp.dot(hit.astype(F32).astype(BF16), upper, preferred_element_type=F32)
    taken = jnp.where(hit & (rank == (row & 7).astype(F32)), (rep & 127).astype(F32) + 1.0, 0.0)
    target = jnp.sum(taken, axis=1, keepdims=True) - 1.0
    place[...] = jnp.where(
        target == lax.broadcasted_iota(I32, (256, 128), 1).astype(F32), 1.0, 0.0).astype(BF16)

    def ag_step(s):
        for k in range(KCH):
            for right in (True, False):
                if s < steps(k, right):
                    ag_wait_recv(k, s, right)
                    if s + 1 < steps(k, right):
                        ag_copy(k, s + 1, right).start()

    def g_wait(kind, h):
        src = {"r": (gr_sem, piece(x + 3, c, h)), "l": (gl_sem, piece(x + 1, c, h)), "f": (gf_sem, piece(x + 2, c, h))}
        sems, ref = src[kind]
        pltpu.make_async_remote_copy(
            src_ref=ref, dst_ref=ref, send_sem=sems.at[0, h], recv_sem=sems.at[1, h],
            device_id=dev(x + 1, y, z, c), device_id_type=MESH).wait_recv()

    def gp_wait(o, h):
        ref = piece(x + o, oc, h)
        pltpu.make_async_remote_copy(
            src_ref=ref, dst_ref=ref, send_sem=gp_sem.at[0, o, h], recv_sem=gp_sem.at[1, o, h],
            device_id=dev(x, y, z, oc), device_id_type=MESH).wait_recv()

    g_wait("r", 0)
    g_forward(0).start()
    g_partner(3, 0).start()
    g_wait("l", 0)
    g_partner(1, 0).start()
    ag_step(0)
    ag_step(1)
    g_wait("l", 1)
    g_forward(1).start()
    g_partner(1, 1).start()
    g_wait("r", 1)
    g_partner(3, 1).start()
    ag_step(2)
    g_wait("f", 0)
    g_partner(2, 0).start()
    ag_step(3)

    def multiply(o):
        xx = lax.rem(x + o, NX)

        def body(zz, total):
            for k in range(KCH):
                total += lax.dot_general(
                    gall[xx, zz, k], pre[k, zz], (((1,), (1,)), ((), ())), preferred_element_type=F32)
            return total

        acc[xx] = lax.fori_loop(0, NZ, body, jnp.zeros((128, 128), F32))

    for o in (0, 1, 3):
        gp_wait(o, 0)
        gp_wait(o, 1)
        multiply(o)
    g_wait("f", 1)
    g_partner(2, 1).start()
    gp_wait(2, 0)
    gp_wait(2, 1)
    multiply(2)

    a2a_s[...] = jnp.dot(
        pack[...], acc[...].reshape(512, 128).astype(BF16), preferred_element_type=F32).astype(BF16).reshape(32, 32, 128)

    def out_copy(o):
        return pltpu.make_async_remote_copy(
            src_ref=a2a_s.at[o], dst_ref=a2a_r.at[own_src], send_sem=as_sem.at[o], recv_sem=ar_sem.at[own_src],
            device_id=owner_of(o), device_id_type=MESH)

    def out_send(i, carry):
        o = lax.rem(d + i, 32)

        @pl.when(o != me_owner)
        def _():
            out_copy(o).start()

        return carry

    lax.fori_loop(0, 32, out_send, 0)

    @pl.when(stays == 1)
    def _():
        a2a_r[own_src] = a2a_s[d]

    def out_wait(s, carry):
        @pl.when(s != me_source)
        def _():
            pltpu.make_async_remote_copy(
                src_ref=a2a_s.at[s], dst_ref=a2a_r.at[s], send_sem=as_sem.at[s], recv_sem=ar_sem.at[s],
                device_id=source_of(s), device_id_type=MESH).wait_recv()

        return carry

    lax.fori_loop(0, 32, out_wait, 0)
    total = jnp.zeros((128, 128), F32)
    for ys in range(NY):
        rows = a2a_r[ys * NZ : (ys + 1) * NZ].reshape(256, 128)
        total += lax.dot_general(place[...], rows, (((0,), (0,)), ((), ())), preferred_element_type=F32)
    out_ref[...] = total

    for k in range(KCH):
        ex_copy(k).wait_send()
        for o in (1, 2, 3):
            rs_copy(k, o).wait_send()

        @pl.when(stays == 0)
        def _():
            tr_copy(k).wait_send()

        for right in (True, False):
            for s in range(steps(k, right)):
                ag_copy(k, s, right).wait_send()
    for h in range(2):
        g_right(h).wait_send()
        g_left(h).wait_send()
        g_forward(h).wait_send()
        for o in range(NX):
            g_partner(o, h).wait_send()

    def drain(i, carry):
        @pl.when(i != me_source)
        def _():
            slot_copy(i).wait_send()

        @pl.when(i != me_owner)
        def _():
            out_copy(i).wait_send()

        return carry

    lax.fori_loop(0, 32, drain, 0)


def local(grads, scales, example_group, group_slot, inv_hess, queries):
    vmem = pl.BlockSpec(memory_space=pltpu.VMEM)
    hbm = pl.BlockSpec(memory_space=pl.ANY)
    dma = pltpu.SemaphoreType.DMA
    return pl.pallas_call(
        kernel,
        out_shape=jax.ShapeDtypeStruct((128, 128), F32),
        in_specs=[hbm, vmem, vmem, vmem, hbm, hbm],
        out_specs=vmem,
        scratch_shapes=[
            pltpu.VMEM((2, 4, 128, 2048), BF16),
            pltpu.VMEM((KCH, 2048, CW), BF16),
            pltpu.VMEM((2, 1024, 1024), BF16),
            pltpu.VMEM((KCH, 4, 128, CW), BF16),
            pltpu.VMEM((KCH, 4, 128, CW), BF16),
            pltpu.VMEM((KCH, 4, 128, CW), F32),
            pltpu.VMEM((KCH, 4, 128, CW), BF16),
            pltpu.VMEM((KCH, 4, 128, CW), BF16),
            pltpu.VMEM((KCH, 128, CW), BF16),
            pltpu.VMEM((KCH, NZ, 128, CW), BF16),
            pltpu.VMEM((NX, NZ, KCH, 128, CW), BF16),
            pltpu.VMEM((NX, 128, 128), F32),
            pltpu.VMEM((32, 1, 128), I32),
            pltpu.VMEM((256, 128), I32),
            pltpu.VMEM((1024, 512), BF16),
            pltpu.VMEM((256, 128), BF16),
            pltpu.VMEM((32, 32, 128), BF16),
            pltpu.VMEM((32, 32, 128), BF16),
            dma((12,)),
            dma((2, KCH)),
            dma((KCH, 4)),
            dma((KCH, 4)),
            dma((2, KCH)),
            dma((2, KCH, 4)),
            dma((2, KCH, 4)),
            dma((2, 2)),
            dma((2, 2)),
            dma((2, 2)),
            dma((2, 4, 2)),
            dma((32,)),
            dma((32,)),
            dma((32,)),
            dma((32,)),
        ],
        compiler_params=pltpu.CompilerParams(collective_id=0, has_side_effects=True, vmem_limit_bytes=48 * 2**20),
        name="scores",
    )(grads, jnp.transpose(scales), example_group, group_slot.reshape(1, 128), inv_hess, queries)


def solution(mesh):
    in_specs = (P("dp", "mp"), P("mp", "dp"), P("dp", None), P("dp"), P("mp", "dp"), P(None, "mp"))
    out_specs = P("dp", "mp")
    return jax.shard_map(local, mesh=mesh, in_specs=in_specs, out_specs=out_specs, check_vma=False)
```

time: 294 us -> 71.7 us (0.24)
  waiting for transfers between devices: 185 us -> 0 us
  Pallas kernels: 0 us -> 66.8 us
  blocking collectives: 47.3 us -> 0 us
  matrix products: 14.5 us -> 0 us
  between operations: 13.5 us -> 0.03 us
  starting transfers between devices: 12.3 us -> 0 us
  local copies, waits for them, and re-layouts: 12.4 us -> 4.59 us
  other arithmetic: 6.37 us -> 0 us
    psum x1 -> x0, waiting for transfers between devices: 162 us -> none  [spread_2(): return lax.psum(kept, axis)]
    pallas_call x0 -> x1, Pallas kernels: none -> 66.8 us  [local(): pl.pallas_call(kernel, out_shape=jax.ShapeDtypeStruct((128, 128), F32), i...]
    all_to_all x2 -> x0, blocking collectives: 47.3 us -> none  [the longest x1 32.5 us: sum_at_owner(): parts = lax.all_to_all(split_up(value, dim, peers), axis, 0, 0, tiled=True)]
    all_to_all x2 -> x0, waiting for transfers between devices: 22.9 us -> none  [the longest x1 15 us: copy_for_each(): return lax.all_to_all(copies, axis, split_axis=0, concat_axis=0, tiled=True)]
    dot_general x2 -> x0, matrix products: 14.5 us -> none  [the longest x1 9.98 us: contract(): lax.dot_general(left, right, (((1,), (1,)), ((), ())), preferred_element_...]
    all_to_all x2 -> x0, starting transfers between devices: 12.3 us -> none  [the longest x1 7.84 us: sum_at_owner(): parts = lax.all_to_all(split_up(value, dim, peers), axis, 0, 0, tiled=True)]
    mul x1 -> x0, local copies, waits for them, and re-layouts: 5.86 us -> none  [local(): grads.reshape(ex_rows, width // QBLOCK, QBLOCK)]
    unnamed x8, local copies, waits for them, and re-layouts: 1.6 us -> 4.59 us
  transfers between devices with their start and end apart: 3 -> 0, of which waited for: 3 -> 0; matrix products, arithmetic and copies ran while one was open for 1% -> 0% of each run, Pallas kernels for 0% -> 0%
where the time goes in v1:
time: 71.7 us; the launch traced here: 71.5 us
  Pallas kernels  66.8 us (93%)
  local copies, waits for them, and re-layouts  4.59 us (6%)
    pallas_call x1, Pallas kernels, local(): pl.pallas_call(kernel, out_shape=jax.ShapeDtypeStruct((128, 128), F32), i...  66.8 us
    unnamed x8, local copies, waits for them, and re-layouts  4.59 us

profile of v1, /device:TPU:1, one launch (start us, length us, event | category | flops | bytes accessed | tf_op | source)
XLA Modules:
  0.0 71.5 jit_solution(11625032610457124246)
XLA Ops:
  0.0 1.0 %copy.7 = f32[16,1024]{0,1:T(8,128)S(1)} copy(f32[16,1024]{1,0:T(8,128)} %param.7) | data formatting | bytes 131072 | tf_op args[1]
  1.0 0.0 copy-start
  1.1 1.6 %copy-done = bf16[2048,512]{1,0:T(8,128)(2,1)S(1)} copy-done((bf16[2048,512]{1,0:T(8,128)(2,1)S(1)}, bf16[2048,512]{1,0:T(8,128)(2,1)}, u32[]{:S(2)}) %copy-start) | copy-done | bytes 2097176
  2.6 0.0 copy-start.1
  2.6 0.7 copy-done.1
  3.3 0.0 copy-start.2
  3.3 0.7 copy-done.2
  4.0 66.8 %scores.1 = f32[128,128]{1,0:T(8,128)S(1)} custom-call(bf16[1024,2048]{1,0:T(8,128)(2,1)} %grads_ref.1, f32[1024,16]{1,0:T(8,128)S(1)} %bitcast.2, s32[1,1024]{1,0:T(1,128)S(1)} %copy-done.1, s32[1,128]{1,0:T(1,128)S(1)} %bitcast.3, bf16[2048,512]{1,0:T(8,128)(2,1)S(1)} %copy-done, bf16[1024,2048]{1,0:T(8,128)(2,1)} %query_ref.1), custom_call_target="tpu_custom_call" | custom-call | tf_op jit(solution)/shard_map/scores/pallas_call | solution.py:415
  70.8 0.6 copy.9
Async XLA Ops:
  1.0 1.6 %copy-start = (bf16[2048,512]{1,0:T(8,128)(2,1)S(1)}, bf16[2048,512]{1,0:T(8,128)(2,1)}, u32[]{:S(2)}) copy-start(bf16[2048,512]{1,0:T(8,128)(2,1)} %hess_ref.1) | copy-start | bytes 6291460
  2.6 0.7 copy-start.1
  3.3 0.7 copy-start.2

commit v2 on v1

--- a/solution.py
+++ b/solution.py
@@ -19,9 +19,9 @@
 
 
 def kernel(
-    grads_ref, sct_ref, member_ref, slot_ref, hess_ref, query_ref, out_ref,
-    q_v, h_v, g_v, ex_s, ex_r, own, rs_s, rs_r, tr_s, pre, gall, acc, slots, slot_rep, pack, place, a2a_s, a2a_r,
-    in_sem, ex_sem, rs_sem, rr_sem, tr_sem, agr_sem, agl_sem, gr_sem, gl_sem, gf_sem, gp_sem, sl_sem, slr_sem, as_sem, ar_sem,
+    grads_ref, scale_ref, member_hbm, slot_hbm, hess_ref, query_ref, out_ref,
+    scale_v, sct_ref, member_ref, slot_ref, q_v, h_v, g_v, ex_s, ex_r, own, rs_s, rs_r, tr_s, pre, gall, acc, slots, slot_rep, pack, place, a2a_s, a2a_r,
+    in_sem, near_sem, ex_sem, rs_sem, rr_sem, tr_sem, agr_sem, agl_sem, gr_sem, gl_sem, gf_sem, gp_sem, sl_sem, slr_sem, as_sem, ar_sem,
 ):
     d = lax.axis_index("dp")
     m = lax.axis_index("mp")
@@ -48,21 +48,26 @@
     for b in range(4):
         q_copy(1, b).start()
     h_copy(1).start()
+    small = [
+        pltpu.make_async_copy(scale_ref, scale_v, in_sem.at[12]),
+        pltpu.make_async_copy(member_hbm, member_ref, in_sem.at[13]),
+        pltpu.make_async_copy(slot_hbm, slot_ref, in_sem.at[14]),
+    ]
+    for copy in small:
+        copy.start()
     g_copy(0).start()
     g_copy(1).start()
 
     barrier = pltpu.get_barrier_semaphore()
 
-    def greet(target):
-        pl.semaphore_signal(barrier, inc=1, device_id=target, device_id_type=MESH)
-
-    greet(dev(x, y, z, oc))
-    for o in (1, 2, 3):
-        greet(dev(x, y + o, z, c))
-    greet(dev(x + 1, y, z, c))
-    greet(dev(x + 3, y, z, c))
-    greet(dev(x, y, z + 1, c))
-    greet(dev(x, y, z + 7, c))
+    def greet(sem, targets):
+        for target in targets:
+            pl.semaphore_signal(sem, inc=1, device_id=target, device_id_type=MESH)
+
+    line_x = [dev(x + o, y, z, c) for o in (2, 1, 3)]
+    line_y = [dev(x, y + o, z, c) for o in (2, 1, 3)]
+    line_z = [dev(x, y, z + o, c) for o in (4, 3, 5, 2, 6, 1, 7)]
+    greet(barrier, line_z + line_y + line_x + [dev(x, y, z, oc)])
 
     def owner_of(o):
         return dev(lax.div(o, NZ), beta, lax.rem(o, NZ), c)
@@ -74,19 +79,6 @@
     own_src = y * NZ + z
     me_owner = jnp.where(stays == 1, d, -1)
     me_source = jnp.where(stays == 1, own_src, -1)
-
-    def greet_32(i, carry):
-        @pl.when(i != me_owner)
-        def _():
-            greet(owner_of(i))
-
-        @pl.when(i != me_source)
-        def _():
-            greet(source_of(i))
-
-        return carry
-
-    lax.fori_loop(0, 32, greet_32, 0)
 
     def partial(i, k):
         return jnp.dot(q_v[i].reshape(512, 2048), h_v[k], preferred_element_type=F32)
@@ -100,7 +92,8 @@
     for b in range(4):
         q_copy(0, b).wait()
     ex_s[0] = partial(0, 0).astype(BF16).reshape(4, 128, CW)
-    pl.semaphore_wait(barrier, 72 - 2 * stays)
+    pl.semaphore_wait(barrier, 14)
+    greet(near_sem.at[0], line_x)
     ex_copy(0).start()
     for b in range(4):
         q_copy(1, b).wait()
@@ -132,24 +125,9 @@
     own[1] = partial(1, 1).reshape(4, 128, CW)
     rs_send(1)
 
-    def slot_copy(s):
-        return pltpu.make_async_remote_copy(
-            src_ref=slot_ref, dst_ref=slots.at[d], send_sem=sl_sem.at[s], recv_sem=slr_sem.at[d],
-            device_id=source_of(s), device_id_type=MESH)
-
-    def slot_send(s, carry):
-        @pl.when(s != me_source)
-        def _():
-            slot_copy(s).start()
-
-        return carry
-
-    lax.fori_loop(0, 32, slot_send, 0)
-
-    @pl.when(stays == 1)
-    def _():
-        slots[d] = slot_ref[...]
-
+    for copy in small:
+        copy.wait()
+    sct_ref[...] = jnp.transpose(scale_v[...])
     onehot = (lax.broadcasted_iota(I32, (128, 1024), 0) == member_ref[...]).astype(F32).astype(BF16)
 
     def group_half(h):
@@ -217,10 +195,31 @@
         def _():
             pre[k, z] = total.astype(BF16)
 
+    pl.semaphore_wait(near_sem.at[0], 3)
+    greet(near_sem.at[1], line_z)
     tr_send(0)
     group_half(1)
     tr_send(1)
     g_send(1)
+
+    def slot_copy(s):
+        return pltpu.make_async_remote_copy(
+            src_ref=slot_ref, dst_ref=slots.at[d], send_sem=sl_sem.at[s], recv_sem=slr_sem.at[d],
+            device_id=source_of(s), device_id_type=MESH)
+
+    def slot_send(s, carry):
+        @pl.when(s != me_source)
+        def _():
+            slot_copy(s).start()
+
+        return carry
+
+    pl.semaphore_wait(near_sem.at[1], 7)
+    lax.fori_loop(0, 32, slot_send, 0)
+
+    @pl.when(stays == 1)
+    def _():
+        slots[d] = slot_ref[...]
 
     def ag_copy(k, s, right):
         sems = agr_sem if right else agl_sem
@@ -246,6 +245,34 @@
 
         ag_copy(k, 0, True).start()
         ag_copy(k, 0, False).start()
+
+    def ag_step(s):
+        for k in range(KCH):
+            for right in (True, False):
+                if s < steps(k, right):
+                    ag_wait_recv(k, s, right)
+                    if s + 1 < steps(k, right):
+                        ag_copy(k, s + 1, right).start()
+
+    def g_wait(kind, h):
+        src = {"r": (gr_sem, piece(x + 3, c, h)), "l": (gl_sem, piece(x + 1, c, h)), "f": (gf_sem, piece(x + 2, c, h))}
+        sems, ref = src[kind]
+        pltpu.make_async_remote_copy(
+            src_ref=ref, dst_ref=ref, send_sem=sems.at[0, h], recv_sem=sems.at[1, h],
+            device_id=dev(x + 1, y, z, c), device_id_type=MESH).wait_recv()
+
+    def gp_wait(o, h):
+        ref = piece(x + o, oc, h)
+        pltpu.make_async_remote_copy(
+            src_ref=ref, dst_ref=ref, send_sem=gp_sem.at[0, o, h], recv_sem=gp_sem.at[1, o, h],
+            device_id=dev(x, y, z, oc), device_id_type=MESH).wait_recv()
+
+    g_wait("r", 0)
+    g_forward(0).start()
+    g_partner(3, 0).start()
+    g_wait("l", 0)
+    g_partner(1, 0).start()
+    ag_step(0)
 
     upper = (lax.broadcasted_iota(I32, (128, 128), 0) < lax.broadcasted_iota(I32, (128, 128), 1)).astype(F32).astype(BF16)
 
@@ -277,33 +304,6 @@
     place[...] = jnp.where(
         target == lax.broadcasted_iota(I32, (256, 128), 1).astype(F32), 1.0, 0.0).astype(BF16)
 
-    def ag_step(s):
-        for k in range(KCH):
-            for right in (True, False):
-                if s < steps(k, right):
-                    ag_wait_recv(k, s, right)
-                    if s + 1 < steps(k, right):
-                        ag_copy(k, s + 1, right).start()
-
-    def g_wait(kind, h):
-        src = {"r": (gr_sem, piece(x + 3, c, h)), "l": (gl_sem, piece(x + 1, c, h)), "f": (gf_sem, piece(x + 2, c, h))}
-        sems, ref = src[kind]
-        pltpu.make_async_remote_copy(
-            src_ref=ref, dst_ref=ref, send_sem=sems.at[0, h], recv_sem=sems.at[1, h],
-            device_id=dev(x + 1, y, z, c), device_id_type=MESH).wait_recv()
-
-    def gp_wait(o, h):
-        ref = piece(x + o, oc, h)
-        pltpu.make_async_remote_copy(
-            src_ref=ref, dst_ref=ref, send_sem=gp_sem.at[0, o, h], recv_sem=gp_sem.at[1, o, h],
-            device_id=dev(x, y, z, oc), device_id_type=MESH).wait_recv()
-
-    g_wait("r", 0)
-    g_forward(0).start()
-    g_partner(3, 0).start()
-    g_wait("l", 0)
-    g_partner(1, 0).start()
-    ag_step(0)
     ag_step(1)
     g_wait("l", 1)
     g_forward(1).start()
@@ -410,14 +410,18 @@
 
 def local(grads, scales, example_group, group_slot, inv_hess, queries):
     vmem = pl.BlockSpec(memory_space=pltpu.VMEM)
-    hbm = pl.BlockSpec(memory_space=pl.ANY)
+    hbm = pl.BlockSpec(memory_space=pltpu.HBM)
     dma = pltpu.SemaphoreType.DMA
     return pl.pallas_call(
         kernel,
         out_shape=jax.ShapeDtypeStruct((128, 128), F32),
-        in_specs=[hbm, vmem, vmem, vmem, hbm, hbm],
+        in_specs=[hbm] * 6,
         out_specs=vmem,
         scratch_shapes=[
+            pltpu.VMEM((16, 1024), F32),
+            pltpu.VMEM((1024, 16), F32),
+            pltpu.VMEM((1, 1024), I32),
+            pltpu.VMEM((1, 128), I32),
             pltpu.VMEM((2, 4, 128, 2048), BF16),
             pltpu.VMEM((KCH, 2048, CW), BF16),
             pltpu.VMEM((2, 1024, 1024), BF16),
@@ -436,7 +440,8 @@
             pltpu.VMEM((256, 128), BF16),
             pltpu.VMEM((32, 32, 128), BF16),
             pltpu.VMEM((32, 32, 128), BF16),
-            dma((12,)),
+            dma((15,)),
+            pltpu.SemaphoreType.REGULAR((2,)),
             dma((2, KCH)),
             dma((KCH, 4)),
             dma((KCH, 4)),
@@ -452,9 +457,9 @@
             dma((32,)),
             dma((32,)),
         ],
-        compiler_params=pltpu.CompilerParams(collective_id=0, has_side_effects=True, vmem_limit_bytes=48 * 2**20),
+        compiler_params=pltpu.CompilerParams(collective_id=0, has_side_effects=True, vmem_limit_bytes=67_043_328),
         name="scores",
-    )(grads, jnp.transpose(scales), example_group, group_slot.reshape(1, 128), inv_hess, queries)
+    )(grads, scales, example_group, group_slot.reshape(1, 128), inv_hess, queries)
 
 
 def solution(mesh):

time: 71.7 us -> 65.6 us (0.915)
  local copies, waits for them, and re-layouts: 4.59 us -> 1.47 us
  Pallas kernels: 66.8 us -> 64 us
    unnamed x8 -> x1, local copies, waits for them, and re-layouts: 4.59 us -> 1.47 us
    pallas_call x1, Pallas kernels: 66.8 us -> 64 us  [local(): pl.pallas_call(kernel, out_shape=jax.ShapeDtypeStruct((128, 128), F32), i...]
where the time goes in v2:
time: 65.6 us; the launch traced here: 65.4 us
  Pallas kernels  64 us (98%)
  local copies, waits for them, and re-layouts  1.47 us (2%)
    pallas_call x1, Pallas kernels, local(): pl.pallas_call(kernel, out_shape=jax.ShapeDtypeStruct((128, 128), F32), i...  64 us
    unnamed x1, local copies, waits for them, and re-layouts  1.47 us

profile of v2, /device:TPU:1, one launch (start us, length us, event | category | flops | bytes accessed | tf_op | source)
XLA Modules:
  0.0 65.4 jit_solution(17355938067405486892)
XLA Ops:
  0.0 64.0 %scores.1 = f32[128,128]{1,0:T(8,128)} custom-call(bf16[1024,2048]{1,0:T(8,128)(2,1)} %grads_ref.1, f32[16,1024]{1,0:T(8,128)} %scale_ref.1, s32[1,1024]{1,0:T(1,128)} %member_hbm.1, s32[1,128]{1,0:T(1,128)} %bitcast.1, bf16[2048,512]{1,0:T(8,128)(2,1)} %hess_ref.1, bf16[1024,2048]{1,0:T(8,128)(2,1)} %query_ref.1), custom_call_target="tpu_custom_call" | custom-call | tf_op jit(solution)/shard_map/scores/pallas_call | solution.py:415
  64.0 1.5 %copy.8 = f32[128,128]{1,0:T(8,128)} copy(f32[128,128]{1,0:T(8,128)} %scores.1) | data formatting | bytes 131072

commit v3 on v2

--- a/solution.py
+++ b/solution.py
@@ -144,7 +144,7 @@
                 gall[x, 4 * c + 2 * h + i, k] = jnp.dot(onehot, deq, preferred_element_type=F32).astype(BF16)
 
     def piece(xx, cc, h):
-        return gall.at[lax.rem(xx, NX), pl.ds(4 * cc + 2 * h, 2)]
+        return gall.at[lax.rem(xx, NX), 4 * cc + h]
 
     def g_right(h):
         return pltpu.make_async_remote_copy(
@@ -157,8 +157,8 @@
             device_id=dev(x + 3, y, z, c), device_id_type=MESH)
 
     def g_forward(h):
-        src = piece(x + 3, c, 0) if h == 0 else piece(x + 1, c, 1)
-        to = dev(x + 1, y, z, c) if h == 0 else dev(x + 3, y, z, c)
+        src = piece(x + 3, c, h) if h < 2 else piece(x + 1, c, h)
+        to = dev(x + 1, y, z, c) if h < 2 else dev(x + 3, y, z, c)
         return pltpu.make_async_remote_copy(
             src_ref=src, dst_ref=src, send_sem=gf_sem.at[0, h], recv_sem=gf_sem.at[1, h], device_id=to, device_id_type=MESH)
 
@@ -174,6 +174,7 @@
 
     group_half(0)
     g_send(0)
+    group_half(1)
 
     def tr_copy(k):
         return pltpu.make_async_remote_copy(
@@ -198,28 +199,9 @@
     pl.semaphore_wait(near_sem.at[0], 3)
     greet(near_sem.at[1], line_z)
     tr_send(0)
-    group_half(1)
     tr_send(1)
-    g_send(1)
-
-    def slot_copy(s):
-        return pltpu.make_async_remote_copy(
-            src_ref=slot_ref, dst_ref=slots.at[d], send_sem=sl_sem.at[s], recv_sem=slr_sem.at[d],
-            device_id=source_of(s), device_id_type=MESH)
-
-    def slot_send(s, carry):
-        @pl.when(s != me_source)
-        def _():
-            slot_copy(s).start()
-
-        return carry
-
-    pl.semaphore_wait(near_sem.at[1], 7)
-    lax.fori_loop(0, 32, slot_send, 0)
-
-    @pl.when(stays == 1)
-    def _():
-        slots[d] = slot_ref[...]
+    for h in (1, 2, 3):
+        g_send(h)
 
     def ag_copy(k, s, right):
         sems = agr_sem if right else agl_sem
@@ -245,6 +227,25 @@
 
         ag_copy(k, 0, True).start()
         ag_copy(k, 0, False).start()
+
+    def slot_copy(s):
+        return pltpu.make_async_remote_copy(
+            src_ref=slot_ref, dst_ref=slots.at[d], send_sem=sl_sem.at[s], recv_sem=slr_sem.at[d],
+            device_id=source_of(s), device_id_type=MESH)
+
+    def slot_send(s, carry):
+        @pl.when(s != me_source)
+        def _():
+            slot_copy(s).start()
+
+        return carry
+
+    pl.semaphore_wait(near_sem.at[1], 7)
+    lax.fori_loop(0, 32, slot_send, 0)
+
+    @pl.when(stays == 1)
+    def _():
+        slots[d] = slot_ref[...]
 
     def ag_step(s):
         for k in range(KCH):
@@ -267,13 +268,48 @@
             src_ref=ref, dst_ref=ref, send_sem=gp_sem.at[0, o, h], recv_sem=gp_sem.at[1, o, h],
             device_id=dev(x, y, z, oc), device_id_type=MESH).wait_recv()
 
-    g_wait("r", 0)
-    g_forward(0).start()
-    g_partner(3, 0).start()
-    g_wait("l", 0)
-    g_partner(1, 0).start()
+    def g_near(h):
+        g_wait("r", h)
+        if h < 2:
+            g_forward(h).start()
+        g_partner(3, h).start()
+        g_wait("l", h)
+        if h >= 2:
+            g_forward(h).start()
+        g_partner(1, h).start()
+
+    def g_far(h):
+        g_wait("f", h)
+        g_partner(2, h).start()
+
+    def multiply(others, blocks, fresh):
+        rows = [lax.rem(x + o, NX) for o in others]
+        left = jnp.concatenate(
+            [jnp.concatenate([gall[xx, zz, k] for zz in blocks for k in range(KCH)], axis=1) for xx in rows], axis=0)
+        right = jnp.concatenate([pre[k, zz] for zz in blocks for k in range(KCH)], axis=1)
+        part = lax.dot_general(left, right, (((1,), (1,)), ((), ())), preferred_element_type=F32)
+        for i, xx in enumerate(rows):
+            piece_of = part[i * 128 : (i + 1) * 128]
+            acc[xx] = piece_of if fresh else acc[xx] + piece_of
+
+    def away(*steps):
+        return [lax.rem(z + r, NZ) for r in steps]
+
+    g_near(0)
+    g_near(1)
     ag_step(0)
-
+    g_near(2)
+    ag_step(1)
+    g_near(3)
+    ag_step(2)
+    for o in (0, 1, 3):
+        for h in range(4):
+            gp_wait(o, h)
+    multiply((0, 1, 3), away(0, 1, 7), True)
+    multiply((0, 1, 3), away(2, 6), False)
+    multiply((0, 1, 3), away(3, 5), False)
+    g_far(0)
+    g_far(2)
     upper = (lax.broadcasted_iota(I32, (128, 128), 0) < lax.broadcasted_iota(I32, (128, 128), 1)).astype(F32).astype(BF16)
 
     def slot_wait(o, carry):
@@ -304,37 +340,16 @@
     place[...] = jnp.where(
         target == lax.broadcasted_iota(I32, (256, 128), 1).astype(F32), 1.0, 0.0).astype(BF16)
 
-    ag_step(1)
-    g_wait("l", 1)
-    g_forward(1).start()
-    g_partner(1, 1).start()
-    g_wait("r", 1)
-    g_partner(3, 1).start()
-    ag_step(2)
-    g_wait("f", 0)
-    g_partner(2, 0).start()
     ag_step(3)
-
-    def multiply(o):
-        xx = lax.rem(x + o, NX)
-
-        def body(zz, total):
-            for k in range(KCH):
-                total += lax.dot_general(
-                    gall[xx, zz, k], pre[k, zz], (((1,), (1,)), ((), ())), preferred_element_type=F32)
-            return total
-
-        acc[xx] = lax.fori_loop(0, NZ, body, jnp.zeros((128, 128), F32))
-
-    for o in (0, 1, 3):
-        gp_wait(o, 0)
-        gp_wait(o, 1)
-        multiply(o)
-    g_wait("f", 1)
-    g_partner(2, 1).start()
-    gp_wait(2, 0)
-    gp_wait(2, 1)
-    multiply(2)
+    multiply((0, 1, 3), away(4), False)
+    for i, h in enumerate((0, 2)):
+        gp_wait(2, h)
+        multiply((2,), (h, 4 + h), i == 0)
+    g_far(1)
+    g_far(3)
+    for h in (1, 3):
+        gp_wait(2, h)
+        multiply((2,), (h, 4 + h), False)
 
     a2a_s[...] = jnp.dot(
         pack[...], acc[...].reshape(512, 128).astype(BF16), preferred_element_type=F32).astype(BF16).reshape(32, 32, 128)
@@ -345,7 +360,10 @@
             device_id=owner_of(o), device_id_type=MESH)
 
     def out_send(i, carry):
-        o = lax.rem(d + i, 32)
+        jx, jz = lax.div(i, NZ), lax.rem(i, NZ)
+        ox = lax.rem(x + 2 + lax.div(jx + 1, 2) * (1 - 2 * lax.rem(jx, 2)), NX)
+        oz = lax.rem(z + 4 + lax.div(jz + 1, 2) * (1 - 2 * lax.rem(jz, 2)), NZ)
+        o = ox * NZ + oz
 
         @pl.when(o != me_owner)
         def _():
@@ -387,7 +405,7 @@
         for right in (True, False):
             for s in range(steps(k, right)):
                 ag_copy(k, s, right).wait_send()
-    for h in range(2):
+    for h in range(4):
         g_right(h).wait_send()
         g_left(h).wait_send()
         g_forward(h).wait_send()
@@ -448,10 +466,10 @@
             dma((2, KCH)),
             dma((2, KCH, 4)),
             dma((2, KCH, 4)),
-            dma((2, 2)),
-            dma((2, 2)),
-            dma((2, 2)),
-            dma((2, 4, 2)),
+            dma((2, 4)),
+            dma((2, 4)),
+            dma((2, 4)),
+            dma((2, 4, 4)),
             dma((32,)),
             dma((32,)),
             dma((32,)),

time: 65.6 us -> 59.3 us (0.904)
  Pallas kernels: 64 us -> 57.7 us
    pallas_call x1, Pallas kernels: 64 us -> 57.7 us  [local(): pl.pallas_call(kernel, out_shape=jax.ShapeDtypeStruct((128, 128), F32), i...]
where the time goes in v3:
time: 59.3 us; the launch traced here: 59.1 us
  Pallas kernels  57.7 us (97%)
  local copies, waits for them, and re-layouts  1.47 us (2%)
    pallas_call x1, Pallas kernels, local(): pl.pallas_call(kernel, out_shape=jax.ShapeDtypeStruct((128, 128), F32), i...  57.7 us
    unnamed x1, local copies, waits for them, and re-layouts  1.47 us

profile of v3, /device:TPU:1, one launch (start us, length us, event | category | flops | bytes accessed | tf_op | source)
XLA Modules:
  0.0 59.1 jit_solution(8548295931551784222)
XLA Ops:
  0.0 57.7 %scores.1 = f32[128,128]{1,0:T(8,128)} custom-call(bf16[1024,2048]{1,0:T(8,128)(2,1)} %grads_ref.1, f32[16,1024]{1,0:T(8,128)} %scale_ref.1, s32[1,1024]{1,0:T(1,128)} %member_hbm.1, s32[1,128]{1,0:T(1,128)} %bitcast.1, bf16[2048,512]{1,0:T(8,128)(2,1)} %hess_ref.1, bf16[1024,2048]{1,0:T(8,128)(2,1)} %query_ref.1), custom_call_target="tpu_custom_call" | custom-call | tf_op jit(solution)/shard_map/scores/pallas_call | solution.py:433
  57.7 1.5 %copy.8 = f32[128,128]{1,0:T(8,128)} copy(f32[128,128]{1,0:T(8,128)} %scores.1) | data formatting | bytes 131072

commit v4 on v3

--- a/solution.py
+++ b/solution.py
@@ -20,8 +20,8 @@
 
 def kernel(
     grads_ref, scale_ref, member_hbm, slot_hbm, hess_ref, query_ref, out_ref,
-    scale_v, sct_ref, member_ref, slot_ref, q_v, h_v, g_v, ex_s, ex_r, own, rs_s, rs_r, tr_s, pre, gall, acc, slots, slot_rep, pack, place, a2a_s, a2a_r,
-    in_sem, near_sem, ex_sem, rs_sem, rr_sem, tr_sem, agr_sem, agl_sem, gr_sem, gl_sem, gf_sem, gp_sem, sl_sem, slr_sem, as_sem, ar_sem,
+    scale_v, sct_ref, member_ref, slot_ref, q_v, h_v, g_v, ex_s, ex_r, own, rs_s, rs_r, tr_s, pre, gall, acc, slots, slot_rep, pack, place, out_s, out_r, mid_s, mid_r,
+    in_sem, near_sem, ex_sem, rs_sem, rr_sem, tr_sem, agr_sem, agl_sem, gr_sem, gl_sem, gf_sem, gp_sem, sl_sem, slr_sem, os_sem, or_sem, ms_sem, mr_sem,
 ):
     d = lax.axis_index("dp")
     m = lax.axis_index("mp")
@@ -69,9 +69,6 @@
     line_z = [dev(x, y, z + o, c) for o in (4, 3, 5, 2, 6, 1, 7)]
     greet(barrier, line_z + line_y + line_x + [dev(x, y, z, oc)])
 
-    def owner_of(o):
-        return dev(lax.div(o, NZ), beta, lax.rem(o, NZ), c)
-
     def source_of(s):
         ys, zs = lax.div(s, NZ), lax.rem(s, NZ)
         return dev(2 * ys - y + NX, ys, zs, c)
@@ -291,6 +288,27 @@
         for i, xx in enumerate(rows):
             piece_of = part[i * 128 : (i + 1) * 128]
             acc[xx] = piece_of if fresh else acc[xx] + piece_of
+
+    def out_copy(o, t):
+        xx, xo = lax.rem(x + o, NX), lax.rem(x + t, NX)
+        return pltpu.make_async_remote_copy(
+            src_ref=out_s.at[xo, xx], dst_ref=out_r.at[y, xx], send_sem=os_sem.at[o, t], recv_sem=or_sem.at[y, xx],
+            device_id=dev(xo, beta, z, c), device_id_type=MESH)
+
+    def packed(o):
+        xx = lax.rem(x + o, NX)
+        rows = jnp.dot(pack[xx], acc[xx].astype(BF16), preferred_element_type=F32)
+        out_s[:, xx] = rows.astype(BF16).reshape(NX, 64, 128)
+        for t in (2, 1, 3):
+            out_copy(o, t).start()
+
+        @pl.when(stays == 0)
+        def _():
+            out_copy(o, 0).start()
+
+        @pl.when(stays == 1)
+        def _():
+            out_r[y, xx] = out_s[x, xx]
 
     def away(*steps):
         return [lax.rem(z + r, NZ) for r in steps]
@@ -322,17 +340,14 @@
         return carry
 
     lax.fori_loop(0, 32, slot_wait, 0)
-    row = lax.broadcasted_iota(I32, (1024, 128), 0)
+    row = lax.broadcasted_iota(I32, (256, 128), 0)
     for xx in range(NX):
-        hit = lax.shift_right_logical(slots[xx * NZ + z], 7) == lax.shift_right_logical(row, 5)
-        mine = hit & ((lax.shift_right_logical(row, 3) & 3) == xx)
+        hit = lax.shift_right_logical(slots[xx * NZ + z], 7) == lax.shift_right_logical(row, 3)
         rank = jnp.dot(hit.astype(F32).astype(BF16), upper, preferred_element_type=F32)
-        pack[:, xx * 128 : (xx + 1) * 128] = jnp.where(
-            mine & (rank == (row & 7).astype(F32)), 1.0, 0.0).astype(BF16)
+        pack[xx] = jnp.where(hit & (rank == (row & 7).astype(F32)), 1.0, 0.0).astype(BF16)
     for j in range(32):
         slot_rep[j * 8 : (j + 1) * 8, :] = jnp.broadcast_to(slots[(j % 4) * NZ + j // 4], (8, 128))
     rep = slot_rep[...]
-    row = lax.broadcasted_iota(I32, (256, 128), 0)
     hit = lax.shift_right_logical(rep, 7) == d
     rank = jnp.dot(hit.astype(F32).astype(BF16), upper, preferred_element_type=F32)
     taken = jnp.where(hit & (rank == (row & 7).astype(F32)), (rep & 127).astype(F32) + 1.0, 0.0)
@@ -342,6 +357,8 @@
 
     ag_step(3)
     multiply((0, 1, 3), away(4), False)
+    for o in (0, 1, 3):
+        packed(o)
     for i, h in enumerate((0, 2)):
         gp_wait(2, h)
         multiply((2,), (h, 4 + h), i == 0)
@@ -351,47 +368,7 @@
         gp_wait(2, h)
         multiply((2,), (h, 4 + h), False)
 
-    a2a_s[...] = jnp.dot(
-        pack[...], acc[...].reshape(512, 128).astype(BF16), preferred_element_type=F32).astype(BF16).reshape(32, 32, 128)
-
-    def out_copy(o):
-        return pltpu.make_async_remote_copy(
-            src_ref=a2a_s.at[o], dst_ref=a2a_r.at[own_src], send_sem=as_sem.at[o], recv_sem=ar_sem.at[own_src],
-            device_id=owner_of(o), device_id_type=MESH)
-
-    def out_send(i, carry):
-        jx, jz = lax.div(i, NZ), lax.rem(i, NZ)
-        ox = lax.rem(x + 2 + lax.div(jx + 1, 2) * (1 - 2 * lax.rem(jx, 2)), NX)
-        oz = lax.rem(z + 4 + lax.div(jz + 1, 2) * (1 - 2 * lax.rem(jz, 2)), NZ)
-        o = ox * NZ + oz
-
-        @pl.when(o != me_owner)
-        def _():
-            out_copy(o).start()
-
-        return carry
-
-    lax.fori_loop(0, 32, out_send, 0)
-
-    @pl.when(stays == 1)
-    def _():
-        a2a_r[own_src] = a2a_s[d]
-
-    def out_wait(s, carry):
-        @pl.when(s != me_source)
-        def _():
-            pltpu.make_async_remote_copy(
-                src_ref=a2a_s.at[s], dst_ref=a2a_r.at[s], send_sem=as_sem.at[s], recv_sem=ar_sem.at[s],
-                device_id=source_of(s), device_id_type=MESH).wait_recv()
-
-        return carry
-
-    lax.fori_loop(0, 32, out_wait, 0)
-    total = jnp.zeros((128, 128), F32)
-    for ys in range(NY):
-        rows = a2a_r[ys * NZ : (ys + 1) * NZ].reshape(256, 128)
-        total += lax.dot_general(place[...], rows, (((0,), (0,)), ((), ())), preferred_element_type=F32)
-    out_ref[...] = total
+    packed(2)
 
     for k in range(KCH):
         ex_copy(k).wait_send()
@@ -417,13 +394,57 @@
         def _():
             slot_copy(i).wait_send()
 
-        @pl.when(i != me_owner)
-        def _():
-            out_copy(i).wait_send()
-
         return carry
 
     lax.fori_loop(0, 32, drain, 0)
+
+    def out_wait(ys):
+        for xx in range(NX):
+            pltpu.make_async_remote_copy(
+                src_ref=out_s.at[0, xx], dst_ref=out_r.at[ys, xx], send_sem=os_sem.at[0, 0], recv_sem=or_sem.at[ys, xx],
+                device_id=dev(2 * ys - y + NX, ys, z, c), device_id_type=MESH).wait_recv()
+
+    for o in (1, 2, 3):
+        out_wait(lax.rem(y + o, NY))
+
+    @pl.when(stays == 0)
+    def _():
+        out_wait(y)
+
+    total = out_r[0].astype(F32)
+    for ys in range(1, NY):
+        total += out_r[ys].astype(F32)
+    total = total.reshape(NX, NZ, 8, 128)
+    for zo in range(NZ):
+        mid_s[zo] = jnp.concatenate([total[xx, zo] for xx in range(NX)], axis=0).astype(BF16)
+
+    def mid_copy(o):
+        zo = lax.rem(z + o, NZ)
+        return pltpu.make_async_remote_copy(
+            src_ref=mid_s.at[zo], dst_ref=mid_r.at[z], send_sem=ms_sem.at[o], recv_sem=mr_sem.at[z],
+            device_id=dev(x, y, z + o, c), device_id_type=MESH)
+
+    for o in (4, 3, 5, 2, 6, 1, 7):
+        mid_copy(o).start()
+    mid_r[z] = mid_s[z]
+    for o in (1, 7, 2, 6, 3, 5, 4):
+        zo = lax.rem(z + o, NZ)
+        pltpu.make_async_remote_copy(
+            src_ref=mid_s.at[zo], dst_ref=mid_r.at[zo], send_sem=ms_sem.at[o], recv_sem=mr_sem.at[zo],
+            device_id=dev(x, y, z + o, c), device_id_type=MESH).wait_recv()
+    out_ref[...] = lax.dot_general(
+        place[...], mid_r[...].reshape(256, 128), (((0,), (0,)), ((), ())), preferred_element_type=F32)
+
+    for o in range(NX):
+        for t in (1, 2, 3):
+            out_copy(o, t).wait_send()
+
+        @pl.when(stays == 0)
+        def _():
+            out_copy(o, 0).wait_send()
+
+    for o in range(1, NZ):
+        mid_copy(o).wait_send()
 
 
 def local(grads, scales, example_group, group_slot, inv_hess, queries):
@@ -454,10 +475,12 @@
             pltpu.VMEM((NX, 128, 128), F32),
             pltpu.VMEM((32, 1, 128), I32),
             pltpu.VMEM((256, 128), I32),
-            pltpu.VMEM((1024, 512), BF16),
+            pltpu.VMEM((NX, 256, 128), BF16),
             pltpu.VMEM((256, 128), BF16),
-            pltpu.VMEM((32, 32, 128), BF16),
-            pltpu.VMEM((32, 32, 128), BF16),
+            pltpu.VMEM((NX, NX, 64, 128), BF16),
+            pltpu.VMEM((NY, NX, 64, 128), BF16),
+            pltpu.VMEM((NZ, 32, 128), BF16),
+            pltpu.VMEM((NZ, 32, 128), BF16),
             dma((15,)),
             pltpu.SemaphoreType.REGULAR((2,)),
             dma((2, KCH)),
@@ -472,8 +495,10 @@
             dma((2, 4, 4)),
             dma((32,)),
             dma((32,)),
-            dma((32,)),
-            dma((32,)),
+            dma((NX, NX)),
+            dma((NY, NX)),
+            dma((NZ,)),
+            dma((NZ,)),
         ],
         compiler_params=pltpu.CompilerParams(collective_id=0, has_side_effects=True, vmem_limit_bytes=67_043_328),
         name="scores",

time: 59.3 us -> 56.9 us (0.960)
  Pallas kernels: 57.7 us -> 55.3 us
    pallas_call x1, Pallas kernels: 57.7 us -> 55.3 us  [local(): pl.pallas_call(kernel, out_shape=jax.ShapeDtypeStruct((128, 128), F32), i...]
where the time goes in v4:
time: 56.9 us; the launch traced here: 56.8 us
  Pallas kernels  55.3 us (97%)
  local copies, waits for them, and re-layouts  1.47 us (3%)
    pallas_call x1, Pallas kernels, local(): pl.pallas_call(kernel, out_shape=jax.ShapeDtypeStruct((128, 128), F32), i...  55.3 us
    unnamed x1, local copies, waits for them, and re-layouts  1.47 us

profile of v4, /device:TPU:1, one launch (start us, length us, event | category | flops | bytes accessed | tf_op | source)
XLA Modules:
  0.0 56.8 jit_solution(6841829141779769460)
XLA Ops:
  0.0 55.3 %scores.1 = f32[128,128]{1,0:T(8,128)} custom-call(bf16[1024,2048]{1,0:T(8,128)(2,1)} %grads_ref.1, f32[16,1024]{1,0:T(8,128)} %scale_ref.1, s32[1,1024]{1,0:T(1,128)} %member_hbm.1, s32[1,128]{1,0:T(1,128)} %bitcast.1, bf16[2048,512]{1,0:T(8,128)(2,1)} %hess_ref.1, bf16[1024,2048]{1,0:T(8,128)(2,1)} %query_ref.1), custom_call_target="tpu_custom_call" | custom-call | tf_op jit(solution)/shard_map/scores/pallas_call | solution.py:454
  55.4 1.5 %copy.8 = f32[128,128]{1,0:T(8,128)} copy(f32[128,128]{1,0:T(8,128)} %scores.1) | data formatting | bytes 131072
